TPU v7x, 32 devices: a whole 2x2x4 slice. The times are simulated.
32 devices in a mesh: order: 1, shard: 32 (over z, y, x, core).
Axes of the slice: x: 2, y: 2, z: 4, core: 2. Of those that a mesh axis runs over, the one named last changes fastest.
Arguments:
- sky_coeffs: float32 [32, 2, 2048], P('shard'), may hold values from -6 to 6
- beam_coeffs: float32 [64, 2048], P('order'), may hold values from -0.09375 to 0.09375
- wigner: bfloat16 [32, 64, 2048, 128], P('shard', 'order'), may hold values from -0.125 to 0.125
- visits: int32 [32, 32, 4], P(('order', 'shard')), may hold values from -1 to 511, as said below
- point_slot: int32 [524288], P(('order', 'shard')), may hold values from 0 to 127, as said below
- phi_cell: int32 [524288], P(('order', 'shard')), may hold values from 0 to 30
- psi_cell: int32 [524288], P(('order', 'shard')), may hold values from 0 to 127
- fraction: float32 [2, 524288], P(None, ('order', 'shard')), may hold values from 0 to 1
Outputs:
- timeline: float32 [524288], P(('order', 'shard'))
Inputs may be any that keep to these rules, and one draw needn't show every extreme that they name: Live entries of one row visits[r, d] are distinct tiles of owner d and come first; every row holds 1 to 4 live entries; for every device r some owner d has all 4 entries live. `point_slot`: every pointing names a live entry of its own device's visit list. Of one device's pointings, exactly 768 name each of half of the owners and 256 each of the others.
All inputs are finite; a program needn't handle non-finite values.
Results may differ from a plain program's by a relative error of at most 0.008.
Values may be sent and summed in bfloat16 or wider, within the bound.
A program may use at most 128 MiB of HBM per device.

v0:
```python
import functools
import math

import jax
import jax.numpy as jnp
import numpy as np
from jax import lax
from jax.experimental import pallas as pl
from jax.experimental.pallas import tpu as pltpu
from jax.sharding import PartitionSpec as P

NPHI = 4096
NPSI = 128
PHI_T = 32
LOW = 8
LANES = 128
CHUNK = 256
KB = 8
BLOCK = 256
F32, BF16, I32 = jnp.float32, jnp.bfloat16, jnp.int32


SQUARE = 4
CORES = 2


def gather_blocks(lines, block_ref, out_ref, send_sem, recv_sem):
    me = lax.axis_index("shard")
    core = me % CORES
    square = me // CORES % SQUARE
    line = me // (CORES * SQUARE)
    depth = block_ref.shape[0]

    def index(at_line, at_square, at_core):
        return (at_line * SQUARE + at_square) * CORES + at_core

    along = [(line + d) % lines for d in range(1, lines)]
    if lines == 4:
        half = line // 2
        along = [line + 1 - 2 * (line % 2), 2 - half, 3 - 3 * half]
    across = [(square + d) % SQUARE for d in range(1, SQUARE)]
    other = (core + 1) % CORES
    line_peers = [index(a, square, core) for a in along]
    square_peers = [index(line, b, core) for b in across]
    twin = index(line, square, other)
    barrier = pltpu.get_barrier_semaphore()
    peers = line_peers + square_peers + [twin]
    for peer in peers:
        pl.semaphore_signal(
            barrier, inc=1, device_id={"shard": peer}, device_id_type=pl.DeviceIdType.MESH
        )
    pl.semaphore_wait(barrier, len(peers))

    started = []

    def place(owner):
        return out_ref.at[pl.ds(pl.multiple_of(owner * depth, depth), depth), :]

    def send(source, owner, peer):
        copy = pltpu.make_async_remote_copy(
            src_ref=source,
            dst_ref=place(owner),
            send_sem=send_sem.at[len(started)],
            recv_sem=recv_sem.at[owner],
            device_id={"shard": peer},
            device_id_type=pl.DeviceIdType.MESH,
        )
        copy.start()
        started.append(copy)

    def arrive(owner):
        pltpu.make_async_remote_copy(
            src_ref=place(owner),
            dst_ref=place(owner),
            send_sem=send_sem.at[0],
            recv_sem=recv_sem.at[owner],
            device_id={"shard": twin},
            device_id_type=pl.DeviceIdType.MESH,
        ).wait_recv()

    for peer in line_peers[::-1] + square_peers + [twin]:
        send(block_ref, me, peer)
    out_ref[pl.ds(pl.multiple_of(me * depth, depth), depth), :] = block_ref[...]
    for owner in line_peers:
        arrive(owner)
        for peer in square_peers + [twin]:
            send(place(owner), owner, peer)
    for a in [line] + along:
        for b in across:
            owner = index(a, b, core)
            arrive(owner)
            send(place(owner), owner, twin)
    for a in [line] + along:
        for b in [square] + across:
            arrive(index(a, b, other))
    for copy in started:
        copy.wait_send()


def wave_table(count, grid, mode):
    phase = 2.0 * math.pi * ((grid * mode) % count) / count
    return np.cos(phase), np.sin(phase)


PARTS = 4
AHEAD = 2
LAG = (3, 5)
NT = (((1,), (1,)), ((), ()))


def grouped(lines, order_count, modes, orders, visits, count, theta):
    owners, depth = visits
    return (
        lines > 1
        and order_count == 1
        and modes == owners
        and orders % KB == 0
        and 2 * orders == theta == owners * depth == PHI_T * depth == NPSI == LANES
        and count % (2 * owners * BLOCK) == 0
        and count == orders * BLOCK
    )


def row_hot(index, size, dtype=BF16):
    n = index.shape[1]
    rows = lax.broadcasted_iota(I32, (size, n), 0)
    if dtype == BF16:
        return rows.astype(F32).astype(BF16) == jnp.broadcast_to(index.astype(F32).astype(BF16), (size, n))
    return rows == index


def pick_row(index, *values):
    size, n = values[0].shape
    totals = [jnp.zeros((8, n), F32) for _ in values]
    index = jnp.broadcast_to(index, (8, n)) - lax.broadcasted_iota(I32, (8, n), 0)
    for r in range(0, size, 8):
        mask = index == r
        totals = [jnp.where(mask, v[r:r + 8], t) for v, t in zip(values, totals)]
    return jnp.sum(functools.reduce(jnp.add, totals), axis=0, keepdims=True)


def block_of(ref, b):
    per = BLOCK // LANES
    return jnp.concatenate([ref[pl.ds(b * per + u, 1), :] for u in range(per)], axis=1)


def mode_order(modes):
    lines = modes // (SQUARE * CORES)
    place = np.arange(modes)
    return (place % lines) * SQUARE * CORES + place // lines % SQUARE * CORES + place // (lines * SQUARE)


def phi_matrix(modes):
    cos, sin = wave_table(NPHI, np.arange(PHI_T)[:, None], mode_order(modes)[None, :])
    core = np.stack([np.stack([cos, -sin], -1), np.stack([sin, cos], -1)], 1)
    full = np.einsum("pamc,kj->pakmcj", core, np.eye(KB))
    return jnp.asarray(full.reshape(PHI_T * 2 * KB, modes * 2 * KB), BF16)


def psi_matrix(orders):
    cos, sin = wave_table(NPSI, np.arange(NPSI)[:, None], np.arange(orders)[None, :])
    pair = np.stack([cos.reshape(NPSI, -1, KB), -sin.reshape(NPSI, -1, KB)], 2)
    return jnp.asarray(pair.reshape(NPSI, 2 * orders), BF16)


def rank_matrix():
    i = np.arange(BLOCK)
    upper = (i[:, None] < i[None, :]).astype(np.float32)
    return jnp.asarray(np.concatenate([upper, np.ones((BLOCK, LANES), np.float32)], 1), BF16)


class Ring:
    def __init__(self, shards, mine, out, send_sem, recv_sem):
        lines = shards // (SQUARE * CORES)
        me = lax.axis_index("shard")
        core, square, line = me % CORES, me // CORES % SQUARE, me // (CORES * SQUARE)
        index = lambda a, b, c: (a * SQUARE + b) * CORES + c
        along = [(line + d) % lines for d in range(1, lines)]
        across = [(square + d) % SQUARE for d in range(1, SQUARE)]
        other = (core + 1) % CORES
        self.shards, self.lines = shards, lines
        self.line_peers = [index(a, square, core) for a in along]
        self.square_peers = [index(line, b, core) for b in across]
        self.twin = index(line, square, other)
        self.all_peers = [
            index(a, b, c) for a in along[::-1] + [line] for b in across[::-1] + [square] for c in (other, core)
        ][:-1]
        self.mine, self.out, self.send_sem, self.recv_sem = mine, out, send_sem, recv_sem
        self.wide = mine.shape[1]
        self.column = core * SQUARE + square
        self.columns = [core * SQUARE + b for b in across]
        self.spot = self.column * lines + line

    def greet(self):
        barrier = pltpu.get_barrier_semaphore()
        for peer in self.all_peers:
            pl.semaphore_signal(barrier, inc=1, device_id={"shard": peer}, device_id_type=pl.DeviceIdType.MESH)
        pl.semaphore_wait(barrier, len(self.all_peers))

    def place(self, j, first, count):
        return self.out.at[j, pl.ds(pl.multiple_of(first * self.wide, self.wide), count * self.wide), :]

    def copy(self, source, target, j, peer, kind):
        return pltpu.make_async_remote_copy(
            src_ref=source,
            dst_ref=target,
            send_sem=self.send_sem.at[j],
            recv_sem=self.recv_sem.at[kind, j],
            device_id={"shard": peer},
            device_id_type=pl.DeviceIdType.MESH,
        )

    def arrive(self, j, kind, blocks):
        span = self.place(j, 0, blocks)
        self.copy(span, span, j, self.twin, kind).wait_recv()

    def sent(self, j, blocks):
        span = self.place(j, 0, blocks)
        self.copy(span, span, j, self.twin, 0).wait_send()

    def first(self, j):
        for peer in self.line_peers:
            self.copy(self.mine.at[j], self.place(j, self.spot, 1), j, peer, 0).start()

    def second(self, j):
        self.arrive(j, 0, self.lines - 1)
        span = self.place(j, self.column * self.lines, self.lines)
        for peer in self.square_peers:
            self.copy(span, span, j, peer, 1).start()
        self.copy(span, span, j, self.twin, 2).start()

    def third(self, j):
        self.arrive(j, 1, (SQUARE - 1) * self.lines)
        for column in self.columns:
            span = self.place(j, column * self.lines, self.lines)
            self.copy(span, span, j, self.twin, 2).start()

    def last(self, j):
        self.arrive(j, 2, SQUARE * self.lines)
        self.sent(j, self.lines - 1)
        self.sent(j, (2 * SQUARE - 1) * self.lines)

    def direct(self, j):
        for peer in self.all_peers:
            self.copy(self.mine.at[j], self.place(j, self.spot, 1), j, peer, 0).start()

    def direct_end(self, j):
        self.arrive(j, 0, self.shards - 1)

    def direct_sent(self, j):
        self.sent(j, self.shards - 1)


def whole_kernel(
    shards, owners, depth,
    sky_hbm, beam_hbm, wigner_hbm, visit_hbm, slot_hbm, phi_hbm, psi_hbm, fraction_hbm, phi_mat_hbm, psi_mat_hbm, rank_hbm,
    out_ref,
    sky, beam, wigner, visit, slot, phi, psi, fraction, phi_mat, psi_mat, rank_mat,
    gathered, mine, turn_cos, turn_sin, dest, carry, chunk_vmem, chunk_smem, moved, hot, weights, aims, synth, lines, table, found, found_both, *rest,
):
    *buffers, load_sem, small_sem, chunk_sem, send_sem, recv_sem = rest
    steps, wide = mine.shape[0], mine.shape[1]
    modes = shards
    theta = wigner.shape[2]
    slots = owners * depth
    blocks = found.shape[0]
    tiles = NPHI // PHI_T
    ring = Ring(shards, mine, gathered, send_sem, recv_sem)

    small = [
        (sky_hbm, sky), (beam_hbm, beam), (slot_hbm, slot), (visit_hbm, visit), (rank_hbm, rank_mat),
        (phi_hbm, phi), (psi_hbm, psi), (fraction_hbm, fraction), (phi_mat_hbm, phi_mat), (psi_mat_hbm, psi_mat),
    ]
    small = [pltpu.make_async_copy(s, d, small_sem.at[n]) for n, (s, d) in enumerate(small)]

    def load(j):
        rows = pl.ds(j * KB, KB)
        return pltpu.make_async_copy(wigner_hbm.at[rows], wigner.at[rows], load_sem.at[j])

    for copy in small[:4]:
        copy.start()
    load(0).start()
    for copy in small[4:]:
        copy.start()
    ahead = AHEAD
    for j in range(1, ahead):
        load(j).start()
    ring.greet()

    small[2].wait()

    def own(b):
        owner = block_of(slot, b) >> int(math.log2(depth))
        return lax.broadcasted_iota(I32, (owners, BLOCK), 0) == owner

    def count(b, total):
        return total + jnp.where(own(b), 1, 0)

    total = lax.fori_loop(0, blocks, count, jnp.zeros((owners, BLOCK), I32), unroll=8)
    held = jnp.broadcast_to(jnp.sum(total, axis=1, keepdims=True), (owners, LANES))
    place = lax.broadcasted_iota(I32, (owners, LANES), 0)
    start = jnp.zeros((owners, LANES), I32)
    for o in range(owners - 1):
        start = start + jnp.where(place > o, jnp.broadcast_to(held[o:o + 1], (owners, LANES)), 0)
    lane = lax.broadcasted_iota(I32, (owners, LANES), 1) * BLOCK
    chunk_vmem[...] = jnp.sum(jnp.where(start + held <= lane, 1, 0), axis=0, keepdims=True)
    carry[...] = start.astype(F32)
    tell = pltpu.make_async_copy(chunk_vmem, chunk_smem, chunk_sem)
    tell.start()

    small[3].wait()
    tile = jnp.maximum(jnp.concatenate([visit[d:d + 1, :] for d in range(depth)], axis=1), 0)
    owner = lax.broadcasted_iota(I32, (1, slots), 1) % owners
    row = owner * (theta // owners) + tile // tiles
    first_phi = (tile % tiles) * PHI_T
    pick = jnp.where(row_hot(row, theta, F32), 1.0, 0.0).astype(BF16)
    spot = lax.broadcasted_iota(I32, (modes, slots), 0)
    n_lines = ring.lines
    mode = (spot % n_lines) * (SQUARE * CORES) + spot // n_lines % SQUARE * CORES + spot // (n_lines * SQUARE)
    angle = ((mode * first_phi) % NPHI).astype(F32) * (2.0 * math.pi / NPHI)
    turn_cos[...] = jnp.cos(angle)
    turn_sin[...] = jnp.sin(angle)
    moved[...] = jnp.zeros_like(moved)
    for copy in small[:2] + small[4:]:
        copy.wait()

    per = blocks // steps

    def rank(i):
        source = jnp.minimum(i, steps - 1)
        masks = [own(source * per + u) for u in range(per)]
        stacked = jnp.concatenate([jnp.where(m, 1.0, 0.0).astype(BF16) for m in masks], axis=0)
        seen = jnp.dot(stacked, rank_mat[...], preferred_element_type=F32)
        base = carry[...]
        for u, mask in enumerate(masks):
            part = seen[u * owners:(u + 1) * owners]
            spots = part[:, :BLOCK] + jnp.concatenate([base] * (BLOCK // LANES), axis=1)
            total = jnp.zeros((8, BLOCK), F32)
            for r in range(0, owners, 8):
                total = jnp.where(mask[r:r + 8], spots[r:r + 8], total)
            dest[pl.ds(i * per + u, 1), :] = jnp.sum(total, axis=0, keepdims=True).astype(I32)
            base = base + part[:, BLOCK:]
        carry[...] = base

    hots = [jnp.ones((BLOCK, BLOCK), BF16), jnp.zeros((BLOCK, BLOCK), BF16)]

    def move(b, to):
        at = block_of(phi, b) * depth + (block_of(slot, b) & (depth - 1))
        mask = row_hot(to >> 8, blocks)
        span = pl.ds(pl.multiple_of(b * BLOCK, BLOCK), BLOCK)
        parts = [at.astype(F32), block_of(psi, b).astype(F32), fraction[0:1, span], fraction[1:2, span]]
        zero = jnp.zeros((blocks, BLOCK), BF16)
        rows = jnp.concatenate(
            [jnp.where(mask, jnp.broadcast_to(p.astype(BF16), (blocks, BLOCK)), zero) for p in parts], axis=0)
        lanes = jnp.where(row_hot(to & 255, BLOCK), *hots)
        hot[span, :] = lanes
        return lax.dot_general(rows, lanes, NT, preferred_element_type=F32)

    size = PHI_T * depth

    def weight(c, s):
        at, along = moved[pl.ds(c, 1), :], moved[pl.ds(2 * blocks + c, 1), :]
        wide_row = lambda w: jnp.broadcast_to(w.astype(BF16), (size, BLOCK))
        both = jnp.where(
            row_hot(at, size), wide_row(1.0 - along),
            jnp.where(row_hot(at + depth, size), wide_row(along), jnp.zeros((size, BLOCK), BF16)))
        weights[pl.ds(pl.multiple_of(c * size, size), size), :] = both
        angle, across = moved[pl.ds(blocks + c, 1), :], moved[pl.ds(3 * blocks + c, 1), :]
        after = jnp.where(angle == NPSI - 1, 0.0, angle + 1.0)
        aims[pl.ds(pl.multiple_of(c * NPSI, NPSI), NPSI), :] = jnp.where(
            row_hot(angle, NPSI), wide_row(1.0 - across),
            jnp.where(row_hot(after, NPSI), wide_row(across), jnp.zeros((NPSI, BLOCK), BF16)))
        return s

    def weigh(j, others):
        part = beam[pl.ds(pl.multiple_of(j * KB, KB), KB), :]
        rows = jnp.concatenate([sky[c:c + 1, :] * part for c in range(2)], axis=0)
        rows = rows.astype(BF16)
        kind = lax.broadcasted_iota(I32, (2 * KB, theta), 0) % KB
        total = jnp.zeros((2 * KB, theta), F32)
        gain = moved[...]
        for kk in range(0, KB, 2):
            pair = jnp.concatenate([wigner[j * KB + kk], wigner[j * KB + kk + 1]], axis=1)
            both = jnp.dot(rows, pair, preferred_element_type=F32)
            for u in range(2):
                total = jnp.where(kind == kk + u, both[:, u * theta:(u + 1) * theta], total)
            for other in others[kk * len(others) // KB:(kk + 2) * len(others) // KB]:
                gain = gain + move(*other)
        moved[...] = gain
        block = total.astype(BF16)
        mine[j] = block
        gathered[j, pl.ds(pl.multiple_of(ring.spot * wide, wide), wide), :] = block

    def synthesize(j, width):
        sides = []
        for w in range(width):
            x = jnp.dot(gathered[j + w], pick, preferred_element_type=F32)
            turned = []
            for m in range(modes):
                re, im = x[m * wide:m * wide + KB], x[m * wide + KB:(m + 1) * wide]
                cm, sm = turn_cos[pl.ds(m, KB, stride=0), :], turn_sin[pl.ds(m, KB, stride=0), :]
                turned.append(jnp.concatenate([cm * re - sm * im, sm * re + cm * im], axis=0).astype(BF16))
            sides.append(jnp.concatenate(turned, axis=0))
        y = jnp.dot(phi_mat[...], jnp.concatenate(sides, axis=1), preferred_element_type=F32)
        for w in range(width):
            for p in range(PHI_T):
                synth[p, pl.ds(pl.multiple_of((j + w) * wide, wide), wide), :] = y[
                    p * wide:(p + 1) * wide, w * slots:(w + 1) * slots].astype(BF16)

    lag = LAG

    def step(i, c):
        load(i).wait()

        @pl.when(i + ahead < steps)
        def _():
            load(i + ahead).start()

        goals = [dest[pl.ds(i * per + u, 1), :] for u in range(per)]
        rank(i + 1)
        weigh(i, [(i * per + u, goal) for u, goal in enumerate(goals)])

        @pl.when(i >= lag[0])
        def _():
            ring.second(i - lag[0])

        @pl.when(i >= lag[1])
        def _():
            ring.third(i - lag[1])

        @pl.when(i < steps - 1)
        def _():
            ring.first(i)

        @pl.when(i == steps - 1)
        def _():
            ring.direct(i)
        return c

    rank(0)
    lax.fori_loop(0, steps, step, 0)
    end = steps - 1
    waits = [(j * 1.5 + 3.75, ring.second, j) for j in range(steps - lag[0], end)]
    waits += [(j * 1.5 + 6.5, ring.third, j) for j in range(steps - lag[1], end)]
    waits.sort(key=lambda w: (w[0], w[2]))
    part = blocks // PARTS
    for n in range(PARTS):
        lax.fori_loop(n * part, (n + 1) * part, weight, 0, unroll=2)
        for _, wait, j in waits[n * len(waits) // PARTS:(n + 1) * len(waits) // PARTS]:
            wait(j)

    def early(j, c):
        ring.last(2 * j)
        ring.last(2 * j + 1)
        synthesize(2 * j, 2)
        return c

    lax.fori_loop(0, end // 2, early, 0)
    if end % 2:
        ring.last(end - 1)
        synthesize(end - 1, 1)
    tell.wait()
    ring.direct_end(end)
    synthesize(end, 1)
    spots = lax.broadcasted_iota(I32, (2 * slots, 2 * slots), 0)
    from_spot = spots // depth % 2 * slots + spots % depth * owners + spots // (2 * depth)
    shuffle = (
        lax.broadcasted_iota(I32, (2 * slots, 2 * slots), 1) == from_spot
    ).astype(F32).astype(BF16)

    def flip(q, c):
        pair = jnp.concatenate([synth[2 * q], synth[2 * q + 1]], axis=1)
        turned = lax.dot_general(shuffle, pair, NT, preferred_element_type=F32)
        rows = 2 * depth
        for o in range(owners):
            lines[pl.ds(pl.multiple_of(o * slots + q * rows, rows), rows), :] = turned[o * rows:(o + 1) * rows]
        return c

    lax.fori_loop(0, PHI_T // 2, flip, 0, unroll=2)

    def cube(p, c):
        part = lines[pl.ds(pl.multiple_of(2 * p * slots, 2 * slots), 2 * slots), :].astype(BF16)
        both = lax.dot_general(psi_mat[...], part, NT, preferred_element_type=F32).astype(BF16)
        for u in range(2):
            table[2 * p + u] = both[:, u * LANES:(u + 1) * LANES]
        return c

    lax.fori_loop(0, owners // 2, cube, 0, unroll=4)
    def meet(c, buffer):
        o = chunk_smem[0, c]
        w = weights[pl.ds(pl.multiple_of(c * size, size), size), :]
        buffer[...] = jnp.dot(table[o], w, preferred_element_type=F32)

    def choose(c, buffer):
        aim = aims[pl.ds(pl.multiple_of(c * NPSI, NPSI), NPSI), :].astype(F32)
        total = jnp.zeros((8, BLOCK), F32)
        for r in range(0, NPSI, 8):
            total = total + buffer[r:r + 8, :] * aim[r:r + 8]
        found[pl.ds(c, 1), :] = jnp.sum(total, axis=0, keepdims=True)

    def pipeline(count, begin, finish, buffers):
        deep = len(buffers) // 2
        for u in range(deep):
            begin(u, buffers[u])

        def both(i, s):
            for side in range(2):
                now = (2 * i + side) * deep
                ahead = jnp.minimum(now + deep, count - deep)
                for u in range(deep):
                    begin(ahead + u, buffers[(1 - side) * deep + u])
                    finish(now + u, buffers[side * deep + u])
            return s

        lax.fori_loop(0, count // (2 * deep), both, 0)

    pipeline(blocks, meet, choose, buffers)
    values = found[...]
    coarse = values.astype(BF16)
    fine = (values - coarse.astype(F32)).astype(BF16)
    found_both[...] = jnp.concatenate([coarse, fine], axis=0)

    def spread(b, buffer):
        lanes = hot[pl.ds(pl.multiple_of(b * BLOCK, BLOCK), BLOCK), :]
        buffer[...] = jnp.dot(found_both[...], lanes, preferred_element_type=F32)

    def settle(b, buffer):
        line = pick_row(dest[pl.ds(b, 1), :] >> 8, buffer.at[0:blocks], buffer.at[blocks:2 * blocks])
        for u in range(BLOCK // LANES):
            out_ref[pl.ds(b * (BLOCK // LANES) + u, 1), :] = line[:, u * LANES:(u + 1) * LANES]

    pipeline(blocks, spread, settle, buffers)
    ring.direct_sent(end)


def run_whole(shards, sky, beam, wigner, visits, point_slot, phi_cell, psi_cell, fraction):
    orders, length, theta = wigner.shape
    owners, depth = visits.shape
    count = point_slot.shape[0]
    blocks = count // BLOCK
    steps, wide = orders // KB, 2 * KB
    slots = owners * depth
    lined = (blocks, BLOCK)
    args = (
        sky, beam, wigner, jnp.transpose(visits), point_slot.reshape(-1, LANES), phi_cell.reshape(-1, LANES),
        psi_cell.reshape(-1, LANES), fraction, phi_matrix(shards), psi_matrix(orders), rank_matrix(),
    )
    return pl.pallas_call(
        functools.partial(whole_kernel, shards, owners, depth),
        out_shape=jax.ShapeDtypeStruct((count // LANES, LANES), F32),
        in_specs=[pl.BlockSpec(memory_space=pl.ANY)] * len(args),
        out_specs=pl.BlockSpec(memory_space=pltpu.VMEM),
        scratch_shapes=[pltpu.VMEM(a.shape, a.dtype) for a in args] + [
            pltpu.VMEM((steps, shards * wide, theta), BF16),
            pltpu.VMEM((steps, wide, theta), BF16),
            pltpu.VMEM((shards, slots), F32),
            pltpu.VMEM((shards, slots), F32),
            pltpu.VMEM((blocks + blocks // steps, BLOCK), I32),
            pltpu.VMEM((owners, LANES), F32),
            pltpu.VMEM((1, LANES), I32),
            pltpu.SMEM((1, LANES), I32),
            pltpu.VMEM((4 * blocks, BLOCK), F32),
            pltpu.VMEM((blocks * BLOCK, BLOCK), BF16),
            pltpu.VMEM((blocks * PHI_T * depth, BLOCK), BF16),
            pltpu.VMEM((blocks * NPSI, BLOCK), BF16),
            pltpu.VMEM((PHI_T, 2 * orders, slots), BF16),
            pltpu.VMEM((PHI_T * slots, 2 * orders), F32),
            pltpu.VMEM((owners, NPSI, LANES), BF16),
            pltpu.VMEM(lined, F32),
            pltpu.VMEM((2 * blocks, BLOCK), BF16),
            *[pltpu.VMEM((max(NPSI, 2 * blocks), BLOCK), F32)] * 8,
            pltpu.SemaphoreType.DMA((steps,)),
            pltpu.SemaphoreType.DMA((len(args) - 1,)),
            pltpu.SemaphoreType.DMA,
            pltpu.SemaphoreType.DMA((steps,)),
            pltpu.SemaphoreType.DMA((3, steps)),
        ],
        compiler_params=pltpu.CompilerParams(collective_id=1, has_side_effects=True, vmem_limit_bytes=67043328),
        name="timeline",
    )(*args).reshape(count)


def interpolate(
    modes,
    orders,
    order_count,
    shard_count,
    coeffs_ref,
    visit_ref,
    phi_table_ref,
    psi_table_ref,
    slot_ref,
    phi_ref,
    psi_ref,
    fraction_ref,
    out_ref,
    picked,
    edge,
    synth,
    wave_a,
    wave_b,
    values_a,
    values_b,
):
    terms = 2 * orders
    high = PHI_T // LOW
    theta = coeffs_ref.shape[1]
    depth, owners = visit_ref.shape
    slots = owners * depth
    blocks = NPHI // (order_count * PHI_T)
    groups = slots // LANES
    listed = jnp.concatenate([visit_ref[d : d + 1, :] for d in range(depth)], axis=1)
    for g in range(groups):
        lanes = slice(g * LANES, (g + 1) * LANES)
        tile = jnp.maximum(listed[:, lanes], 0)
        owner = (lax.broadcasted_iota(jnp.int32, (1, LANES), 1) + g * LANES) % owners
        row = (owner % shard_count) * (theta // shard_count) + tile // blocks
        first_phi = (owner // shard_count) * (NPHI // order_count) + (tile % blocks) * PHI_T
        chosen = (
            lax.broadcasted_iota(jnp.int32, (theta, LANES), 0) == row
        ).astype(jnp.float32).astype(jnp.bfloat16)

        def pick(m, carry):
            rows = pl.ds(pl.multiple_of(m * 4 * terms, 4 * terms), 4 * terms)
            picked[rows, :] = jnp.dot(
                coeffs_ref[rows, :], chosen, preferred_element_type=jnp.float32
            )
            return carry

        lax.fori_loop(0, modes // 4, pick, 0)
        turn = (lax.broadcasted_iota(jnp.int32, (modes, LANES), 0) * first_phi) % NPHI
        angle = turn.astype(jnp.float32) * (2.0 * math.pi / NPHI)
        turn_cos, turn_sin = jnp.cos(angle), jnp.sin(angle)

        def sum_modes(k, carry):
            real = picked[pl.ds(2 * k, modes, stride=terms), :]
            imag = picked[pl.ds(2 * k + 1, modes, stride=terms), :]
            turned = jnp.concatenate(
                [turn_cos * real - turn_sin * imag, turn_sin * real + turn_cos * imag], axis=0
            ).astype(jnp.bfloat16)
            values = jnp.dot(phi_table_ref[...], turned, preferred_element_type=jnp.float32)
            for h in range(high):
                synth[
                    pl.ds(pl.multiple_of(k * 2 * LOW, 2 * LOW), 2 * LOW),
                    h * slots + g * LANES : h * slots + (g + 1) * LANES,
                ] = values[h * 2 * LOW : (h + 1) * 2 * LOW].astype(jnp.bfloat16)
            edge[pl.ds(pl.multiple_of(k * 2 * high, 2 * high), 2 * high), :] = values[
                2 * PHI_T :
            ]
            return carry

        lax.fori_loop(0, orders, sum_modes, 0, unroll=4)
        for part in range(2):
            for h in range(high):
                synth[
                    terms * LOW + part * orders : terms * LOW + (part + 1) * orders,
                    h * slots + g * LANES : h * slots + (g + 1) * LANES,
                ] = edge[pl.ds(part * high + h, orders, stride=2 * high), :].astype(jnp.bfloat16)

    def begin(i, values, wave):
        phi, psi = phi_ref[i], psi_ref[i]
        along_psi = fraction_ref[i][1:2]
        slot = slot_ref[i]
        key = ((phi // LOW) * depth + slot % depth) * owners + slot // depth
        entry = (
            lax.broadcasted_iota(jnp.int32, (high * slots, CHUNK), 0) == key
        ).astype(jnp.float32).astype(jnp.bfloat16)
        at_psi = lax.broadcasted_iota(jnp.int32, (NPSI, CHUNK), 0)
        weight = jnp.where(
            at_psi == psi, 1.0 - along_psi, jnp.where(at_psi == (psi + 1) % NPSI, along_psi, 0.0)
        )
        coarse = weight.astype(jnp.bfloat16)
        fine = (weight - coarse.astype(jnp.float32)).astype(jnp.bfloat16)
        wave[...] = jnp.dot(
            psi_table_ref[...],
            jnp.concatenate([coarse, fine], axis=0),
            preferred_element_type=jnp.float32,
        )
        values[...] = jnp.dot(synth[...], entry, preferred_element_type=jnp.float32)

    def finish(i, values, wave):
        phi = phi_ref[i]
        along_phi = fraction_ref[i][0:1]
        sums = [jnp.zeros((LOW, CHUNK), jnp.float32) for _ in range(4)]
        for k in range(orders):
            for part in range(2):
                at = (2 * k + part) * LOW
                line = part * orders + k
                sums[at // LOW % 4] += values[at : at + LOW, :] * wave[line : line + 1, :]
        inner = (sums[0] + sums[1]) + (sums[2] + sums[3])
        last = jnp.sum(values[terms * LOW :, :] * wave[...], axis=0, keepdims=True)
        low = phi % LOW
        at_low = lax.broadcasted_iota(jnp.int32, (LOW, CHUNK), 0)
        weight_phi = jnp.where(
            at_low == low, 1.0 - along_phi, jnp.where(at_low == low + 1, along_phi, 0.0)
        )
        total = jnp.sum(inner * weight_phi, axis=0, keepdims=True)
        out_ref[i] = total + jnp.where(low == LOW - 1, along_phi, 0.0) * last

    chunks = slot_ref.shape[0]
    begin(0, values_a, wave_a)

    def pair(i, carry):
        begin(2 * i + 1, values_b, wave_b)
        finish(2 * i, values_a, wave_a)
        begin(jnp.minimum(2 * i + 2, chunks - 1), values_a, wave_a)
        finish(2 * i + 1, values_b, wave_b)
        return carry

    lax.fori_loop(0, chunks // 2, pair, 0)


def phi_rows(modes):
    mode = np.arange(modes, dtype=np.int64)[None, :]
    high = PHI_T // LOW
    cos, sin = wave_table(NPHI, np.arange(PHI_T, dtype=np.int64)[:, None], mode)
    real = np.concatenate([cos, -sin], axis=1)
    imag = np.concatenate([sin, cos], axis=1)
    inner = np.stack(
        [real.reshape(high, LOW, 2 * modes), imag.reshape(high, LOW, 2 * modes)], axis=1
    ).reshape(2 * PHI_T, 2 * modes)
    zero = np.zeros((1, 2 * modes), np.float64)
    edge = np.concatenate([real[LOW::LOW], zero, imag[LOW::LOW], zero], axis=0)
    return jnp.asarray(np.concatenate([inner, edge], axis=0), jnp.bfloat16)


def psi_rows(orders):
    order = np.arange(orders, dtype=np.int64)[:, None]
    cos, sin = wave_table(NPSI, np.arange(NPSI, dtype=np.int64)[None, :], order)
    half = np.concatenate([cos, -sin], axis=0)
    return jnp.asarray(np.concatenate([half, half], axis=1), jnp.bfloat16)


def shards(sky_coeffs, beam_coeffs, wigner, visits, point_slot, phi_cell, psi_cell, fraction):
    order_count = lax.axis_size("order")
    shard_count = lax.axis_size("shard")
    local_modes = sky_coeffs.shape[0]
    local_orders = beam_coeffs.shape[0]
    theta_count = wigner.shape[3]
    orders = local_orders * order_count
    modes = local_modes * shard_count
    lines = shard_count // (SQUARE * CORES)
    if grouped(lines, order_count, modes, orders, visits.shape[1:], point_slot.shape[0], theta_count):
        return run_whole(
            shard_count, sky_coeffs[0], beam_coeffs, wigner[0], visits[0], point_slot, phi_cell, psi_cell, fraction
        )
    weighted = (sky_coeffs[:, None, :, :] * beam_coeffs[None, :, None, :]).astype(jnp.bfloat16)
    coeffs = jnp.einsum("mkcl,mklt->mkct", weighted, wigner, preferred_element_type=jnp.float32)
    coeffs = coeffs.astype(jnp.bfloat16).reshape(local_modes * local_orders * 2, theta_count)
    coeffs = pl.pallas_call(
        functools.partial(gather_blocks, shard_count // (SQUARE * CORES)),
        out_shape=jax.ShapeDtypeStruct((shard_count * coeffs.shape[0], theta_count), jnp.bfloat16),
        in_specs=[pl.BlockSpec(memory_space=pltpu.VMEM)],
        out_specs=pl.BlockSpec(memory_space=pltpu.VMEM),
        scratch_shapes=[
            pltpu.SemaphoreType.DMA((shard_count - 1,)),
            pltpu.SemaphoreType.DMA((shard_count,)),
        ],
        compiler_params=pltpu.CompilerParams(collective_id=0, has_side_effects=True),
    )(coeffs)
    if order_count > 1:
        coeffs = coeffs.reshape(modes, local_orders * 2, theta_count)
        coeffs = lax.all_gather(coeffs, "order", axis=1, tiled=True)
        coeffs = coeffs.reshape(modes * orders * 2, theta_count)

    slots = visits.shape[1] * visits.shape[2]
    count = point_slot.shape[0]
    chunks = count // CHUNK
    lined = (chunks, 1, CHUNK)
    pairs = jnp.transpose(fraction.reshape(2, chunks, CHUNK), (1, 0, 2))
    high = PHI_T // LOW
    timeline = pl.pallas_call(
        functools.partial(
            interpolate, modes, orders, order_count, shard_count
        ),
        out_shape=jax.ShapeDtypeStruct(lined, jnp.float32),
        in_specs=[pl.BlockSpec(memory_space=pltpu.VMEM)] * 8,
        out_specs=pl.BlockSpec(memory_space=pltpu.VMEM),
        scratch_shapes=[
            pltpu.VMEM((modes * orders * 2, LANES), jnp.float32),
            pltpu.VMEM((orders * 2 * high, LANES), jnp.float32),
            pltpu.VMEM((orders * 2 * (LOW + 1), high * slots), jnp.bfloat16),
            pltpu.VMEM((orders * 2, CHUNK), jnp.float32),
            pltpu.VMEM((orders * 2, CHUNK), jnp.float32),
            pltpu.VMEM((orders * 2 * (LOW + 1), CHUNK), jnp.float32),
            pltpu.VMEM((orders * 2 * (LOW + 1), CHUNK), jnp.float32),
        ],
    )(
        coeffs,
        jnp.transpose(visits[0]),
        phi_rows(modes),
        psi_rows(orders),
        point_slot.reshape(lined),
        phi_cell.reshape(lined),
        psi_cell.reshape(lined),
        pairs,
    )
    return timeline.reshape(count)


def solution(mesh):
    placed = (
        P("shard", None, None),
        P("order", None),
        P("shard", "order", None, None),
        P(("order", "shard"), None, None),
        P(("order", "shard")),
        P(("order", "shard")),
        P(("order", "shard")),
        P(None, ("order", "shard")),
    )
    return jax.shard_map(
        shards, mesh=mesh, in_specs=placed, out_specs=P(("order", "shard")), check_vma=False
    )
```

profile of v0, /device:TPU:0, one launch (start us, length us, event | category | flops | bytes accessed | tf_op | source)
XLA Modules:
  0.0 38.6 jit_solution(10826613508085973391)
XLA Ops:
  0.0 37.1 %timeline.1 = f32[128,128]{1,0:T(8,128)} custom-call(f32[2,2048]{1,0:T(2,128)} %bitcast.14, f32[64,2048]{1,0:T(8,128)} %beam_hbm.1, bf16[64,2048,128]{2,1,0:T(8,128)(2,1)} %bitcast.9, s32[4,32]{1,0:T(4,128)} %bitcast.15, s32[128,128]{1,0:T(8,128)} %bitcast.11, s32[128,128]{1,0:T(8,128)} %bitcast.12, s32[128,128]{1,0:T(8,128)} %bitcast.13, ...), custom_call_target="tpu_custom_call" | custom-call | tf_op jit(solution)/shard_map/timeline/pallas_call | solution.py:548
  37.1 1.5 %copy.13 = f32[16384]{0:T(1024)} copy(f32[16384]{0:T(1024)} %bitcast.10) | data formatting | bytes 131072
where the time goes:
time: 38.8 us; the launch traced here: 38.6 us
  Pallas kernels  37.1 us (96%)
  local copies, waits for them, and re-layouts  1.47 us (4%)
    pallas_call x1, Pallas kernels, run_whole(): pl.pallas_call(functools.partial(whole_kernel, shards, owners, depth), ou...  37.1 us
    unnamed x1, local copies, waits for them, and re-layouts  1.47 us

commit v1 on v0

--- a/solution.py
+++ b/solution.py
@@ -102,6 +102,9 @@
     return np.cos(phase), np.sin(phase)
 
 
+INSIDE = True
+EARLY = True
+FINE = True
 PARTS = 4
 AHEAD = 2
 LAG = (3, 5)
@@ -191,11 +194,13 @@
         self.columns = [core * SQUARE + b for b in across]
         self.spot = self.column * lines + line
 
-    def greet(self):
+    def hail(self):
         barrier = pltpu.get_barrier_semaphore()
         for peer in self.all_peers:
             pl.semaphore_signal(barrier, inc=1, device_id={"shard": peer}, device_id_type=pl.DeviceIdType.MESH)
-        pl.semaphore_wait(barrier, len(self.all_peers))
+
+    def meet(self):
+        pl.semaphore_wait(pltpu.get_barrier_semaphore(), len(self.all_peers))
 
     def place(self, j, first, count):
         return self.out.at[j, pl.ds(pl.multiple_of(first * self.wide, self.wide), count * self.wide), :]
@@ -283,9 +288,10 @@
     for copy in small[4:]:
         copy.start()
     ahead = AHEAD
-    for j in range(1, ahead):
-        load(j).start()
-    ring.greet()
+    if EARLY:
+        for j in range(1, ahead):
+            load(j).start()
+    ring.hail()
 
     small[2].wait()
 
@@ -420,6 +426,11 @@
         rank(i + 1)
         weigh(i, [(i * per + u, goal) for u, goal in enumerate(goals)])
 
+        if INSIDE:
+            @pl.when(i == 0)
+            def _():
+                ring.meet()
+
         @pl.when(i >= lag[0])
         def _():
             ring.second(i - lag[0])
@@ -437,7 +448,12 @@
             ring.direct(i)
         return c
 
+    if not EARLY:
+        for j in range(1, ahead):
+            load(j).start()
     rank(0)
+    if not INSIDE:
+        ring.meet()
     lax.fori_loop(0, steps, step, 0)
     end = steps - 1
     waits = [(j * 1.5 + 3.75, ring.second, j) for j in range(steps - lag[0], end)]
@@ -469,14 +485,18 @@
     ).astype(F32).astype(BF16)
 
     def flip(q, c):
-        pair = jnp.concatenate([synth[2 * q], synth[2 * q + 1]], axis=1)
-        turned = lax.dot_general(shuffle, pair, NT, preferred_element_type=F32)
+        pairs = [
+            jnp.concatenate([synth[4 * q + 2 * u], synth[4 * q + 2 * u + 1]], axis=1) for u in range(2)
+        ]
+        turned = lax.dot_general(shuffle, jnp.concatenate(pairs, axis=0), NT, preferred_element_type=F32)
         rows = 2 * depth
         for o in range(owners):
-            lines[pl.ds(pl.multiple_of(o * slots + q * rows, rows), rows), :] = turned[o * rows:(o + 1) * rows]
+            for u in range(2):
+                lines[pl.ds(pl.multiple_of(o * slots + (2 * q + u) * rows, rows), rows), :] = turned[
+                    o * rows:(o + 1) * rows, u * LANES:(u + 1) * LANES]
         return c
 
-    lax.fori_loop(0, PHI_T // 2, flip, 0, unroll=2)
+    lax.fori_loop(0, PHI_T // 4, flip, 0, unroll=2)
 
     def cube(p, c):
         part = lines[pl.ds(pl.multiple_of(2 * p * slots, 2 * slots), 2 * slots), :].astype(BF16)
@@ -485,7 +505,7 @@
             table[2 * p + u] = both[:, u * LANES:(u + 1) * LANES]
         return c
 
-    lax.fori_loop(0, owners // 2, cube, 0, unroll=4)
+    lax.fori_loop(0, owners // 2, cube, 0, unroll=8)
     def meet(c, buffer):
         o = chunk_smem[0, c]
         w = weights[pl.ds(pl.multiple_of(c * size, size), size), :]
@@ -517,15 +537,19 @@
     pipeline(blocks, meet, choose, buffers)
     values = found[...]
     coarse = values.astype(BF16)
-    fine = (values - coarse.astype(F32)).astype(BF16)
-    found_both[...] = jnp.concatenate([coarse, fine], axis=0)
+    if FINE:
+        found_both[...] = jnp.concatenate([coarse, (values - coarse.astype(F32)).astype(BF16)], axis=0)
+    else:
+        found_both[0:blocks] = coarse
 
     def spread(b, buffer):
         lanes = hot[pl.ds(pl.multiple_of(b * BLOCK, BLOCK), BLOCK), :]
-        buffer[...] = jnp.dot(found_both[...], lanes, preferred_element_type=F32)
+        height = 2 * blocks if FINE else blocks
+        buffer[0:height] = jnp.dot(found_both[0:height], lanes, preferred_element_type=F32)
 
     def settle(b, buffer):
-        line = pick_row(dest[pl.ds(b, 1), :] >> 8, buffer.at[0:blocks], buffer.at[blocks:2 * blocks])
+        parts = [buffer.at[0:blocks], buffer.at[blocks:2 * blocks]] if FINE else [buffer.at[0:blocks]]
+        line = pick_row(dest[pl.ds(b, 1), :] >> 8, *parts)
         for u in range(BLOCK // LANES):
             out_ref[pl.ds(b * (BLOCK // LANES) + u, 1), :] = line[:, u * LANES:(u + 1) * LANES]
 

time: 38.8 us -> 36.4 us (0.938)
  Pallas kernels: 37.1 us -> 34.7 us
    pallas_call x1, Pallas kernels: 37.1 us -> 34.7 us  [run_whole(): pl.pallas_call(functools.partial(whole_kernel, shards, owners, depth), ou...]
where the time goes in v1:
time: 36.4 us; the launch traced here: 36.2 us
  Pallas kernels  34.7 us (95%)
  local copies, waits for them, and re-layouts  1.47 us (4%)
    pallas_call x1, Pallas kernels, run_whole(): pl.pallas_call(functools.partial(whole_kernel, shards, owners, depth), ou...  34.7 us
    unnamed x1, local copies, waits for them, and re-layouts  1.47 us

profile of v1, /device:TPU:0, one launch (start us, length us, event | category | flops | bytes accessed | tf_op | source)
XLA Modules:
  0.0 36.2 jit_solution(12667256274560904938)
XLA Ops:
  0.0 34.7 %timeline.1 = f32[128,128]{1,0:T(8,128)} custom-call(f32[2,2048]{1,0:T(2,128)} %bitcast.14, f32[64,2048]{1,0:T(8,128)} %beam_hbm.1, bf16[64,2048,128]{2,1,0:T(8,128)(2,1)} %bitcast.9, s32[4,32]{1,0:T(4,128)} %bitcast.15, s32[128,128]{1,0:T(8,128)} %bitcast.11, s32[128,128]{1,0:T(8,128)} %bitcast.12, s32[128,128]{1,0:T(8,128)} %bitcast.13, ...), custom_call_target="tpu_custom_call" | custom-call | tf_op jit(solution)/shard_map/timeline/pallas_call | solution.py:572
  34.8 1.5 %copy.13 = f32[16384]{0:T(1024)} copy(f32[16384]{0:T(1024)} %bitcast.10) | data formatting | bytes 131072

commit v2 on v1

--- a/solution.py
+++ b/solution.py
@@ -461,7 +461,7 @@
     waits.sort(key=lambda w: (w[0], w[2]))
     part = blocks // PARTS
     for n in range(PARTS):
-        lax.fori_loop(n * part, (n + 1) * part, weight, 0, unroll=2)
+        lax.fori_loop(n * part, (n + 1) * part, weight, 0, unroll=4)
         for _, wait, j in waits[n * len(waits) // PARTS:(n + 1) * len(waits) // PARTS]:
             wait(j)
 

time: 36.4 us -> 36.4 us (level)
  no operation moved by 1% of the time
where the time goes in v2:
time: 36.4 us; the launch traced here: 36.2 us
  Pallas kernels  34.7 us (95%)
  local copies, waits for them, and re-layouts  1.47 us (4%)
    pallas_call x1, Pallas kernels, run_whole(): pl.pallas_call(functools.partial(whole_kernel, shards, owners, depth), ou...  34.7 us
    unnamed x1, local copies, waits for them, and re-layouts  1.47 us

profile of v2, /device:TPU:0, one launch (start us, length us, event | category | flops | bytes accessed | tf_op | source)
XLA Modules:
  0.0 36.2 jit_solution(8746554422799793910)
XLA Ops:
  0.0 34.7 %timeline.1 = f32[128,128]{1,0:T(8,128)} custom-call(f32[2,2048]{1,0:T(2,128)} %bitcast.14, f32[64,2048]{1,0:T(8,128)} %beam_hbm.1, bf16[64,2048,128]{2,1,0:T(8,128)(2,1)} %bitcast.9, s32[4,32]{1,0:T(4,128)} %bitcast.15, s32[128,128]{1,0:T(8,128)} %bitcast.11, s32[128,128]{1,0:T(8,128)} %bitcast.12, s32[128,128]{1,0:T(8,128)} %bitcast.13, ...), custom_call_target="tpu_custom_call" | custom-call | tf_op jit(solution)/shard_map/timeline/pallas_call | solution.py:572
  34.7 1.5 %copy.13 = f32[16384]{0:T(1024)} copy(f32[16384]{0:T(1024)} %bitcast.10) | data formatting | bytes 131072
